TPU v7x, 256 devices: a whole 4x4x8 slice. The times are simulated.
256 devices in a mesh: loop: 4 (over x_lo, core), sub: 64 (over z, y, x_hi).
Axes of the slice: x: 4 (x_hi: 2, x_lo: 2; x = x_hi * 2 + x_lo), y: 4, z: 8, core: 2. Of those that a mesh axis runs over, the one named last changes fastest.
Arguments:
- rate: float32 [8192, 5, 384], P(('loop', 'sub')), may hold values from 0 to 1
- phase: float32 [8192, 5, 384], P(('loop', 'sub')), may hold values from -3.140625 to 3.140625
- forcing: float32 [2, 4, 8192, 5, 384], P(None, None, ('loop', 'sub')), may hold values from -8 to 8
Outputs:
- response: float32 [2, 4, 8192, 5, 384], P(None, None, ('loop', 'sub'))
All inputs are finite; a program needn't handle non-finite values.
Results may differ from a plain program's by a relative error of at most 0.0003.
Values sent between devices are 32-bit elements; how exact they have to be, the bound alone decides.
A program may use at most 128 MiB of HBM per device.

v0:
```python
import jax
import jax.numpy as jnp
from jax import lax
from jax.sharding import PartitionSpec as P

fringe_total = 0.7


def carried_in(value, axis, join, neutral):
    count, mine = (lax.axis_size(axis), lax.axis_index(axis))
    pieces = jax.tree.map(lambda part: lax.all_gather(part, axis), value)
    subtotal = jax.tree.map(
        lambda part, zero: jnp.full_like(part, 0) + jnp.asarray(zero, part.dtype), value, neutral
    )

    def hop(position, subtotal):
        longer = join(subtotal, jax.tree.map(lambda part: part[position], pieces))
        return jax.tree.map(lambda new, old: jnp.where(position < mine, new, old), longer, subtotal)

    return lax.fori_loop(0, count - 1, hop, subtotal)


def broadcast(value, axis, source):
    kept = jnp.where(lax.axis_index(axis) == source, value, 0).astype(value.dtype)
    return lax.psum(kept, axis)


def complex_product(left, right):
    return jnp.stack(
        [left[0] * right[0] - left[1] * right[1], left[0] * right[1] + left[1] * right[0]]
    )


def compose(earlier, later):
    return (complex_product(later[0], earlier[0]), complex_product(later[0], earlier[1]) + later[1])


def local(rate, phase, forcing):
    stations = rate.shape[0]
    devices = lax.axis_size(("loop", "sub"))
    is_last = lax.axis_index(("loop", "sub")) == devices - 1
    fringe_sponge = jnp.where(
        is_last, jnp.float32(fringe_total ** (1.0 / stations)), jnp.float32(1.0)
    )
    magnitude = jnp.exp(-rate) * fringe_sponge
    coeff = jnp.stack([magnitude * jnp.cos(phase), magnitude * jnp.sin(phase)])[:, None]
    source = jnp.sqrt(-jnp.expm1(-2.0 * rate)) * forcing
    local_a, local_b = lax.associative_scan(compose, (coeff, source), axis=2)
    own = (local_a[:, :, -1], local_b[:, :, -1])
    unit = (
        jnp.stack([jnp.ones_like(own[0][0]), jnp.zeros_like(own[0][0])]),
        jnp.zeros_like(own[1]),
    )
    before = carried_in((own[0], own[1]), ("loop", "sub"), compose, unit)
    through = compose(before, own)
    circuit_transfer = (
        broadcast(through[0], ("loop", "sub"), devices - 1),
        broadcast(through[1], ("loop", "sub"), devices - 1),
    )
    denom_re = 1.0 - circuit_transfer[0][0]
    denom_im = -circuit_transfer[0][1]
    scale = denom_re * denom_re + denom_im * denom_im
    closing = complex_product(circuit_transfer[1], jnp.stack([denom_re, -denom_im])) / scale
    entering = complex_product(before[0], closing) + before[1]
    return local_b + complex_product(local_a, entering[:, :, None])


def solution(mesh):
    placed = (
        P(("loop", "sub"), None, None),
        P(("loop", "sub"), None, None),
        P(None, None, ("loop", "sub"), None, None),
    )
    return jax.shard_map(
        local,
        mesh=mesh,
        in_specs=placed,
        out_specs=P(None, None, ("loop", "sub"), None, None),
        check_vma=False,
    )
```

profile of v0, /device:TPU:1, one launch (start us, length us, event | category | flops | bytes accessed | tf_op | source)
XLA Modules:
  0.0 2151.6 jit_solution(167800945347909830)
XLA Ops:
  6.5 2.1 multiply_bitcast_fusion.1
  14.3 2.9 copy_multiply_fusion
  22.9 7.1 pad.65
  31.4 14.1 pad.67
  46.3 1.1 multiply_subtract_fusion.9
  47.4 1.0 maximum_add_fusion.7
  49.2 18.9 pad.66
  68.1 2.0 add.312
  70.0 1.3 multiply_subtract_fusion.5
  71.5 0.9 pad_maximum_fusion.1
  72.4 28.2 %pad.68 = f32[2,4,16,5,384]{4,1,3,2,0:T(4,128)S(1)} pad(f32[2,4,8,5,384]{4,1,3,2,0:T(4,128)} %pad_maximum_fusion.1, f32[]{:T(128)} %constant.47.clone.1), padding=0_0_0x0_0_0x0_1_1x0_0_0x0_0_0 | pad | bytes 1474564 | tf_op jit(solution)/shard_map/pad | solution.py:48
  100.6 25.2 %pad.69 = f32[2,4,16,5,384]{4,1,3,2,0:T(4,128)} pad(f32[2,4,8,5,384]{4,1,3,2,0:T(4,128)S(1)} %copy-done.7, f32[]{:T(128)} %constant.47.clone.1), padding=0_0_0x0_0_0x1_0_1x0_0_0x0_0_0 | pad | bytes 1474564 | tf_op jit(solution)/shard_map/pad | solution.py:48
  125.8 2.4 add.315
  128.2 71.2 %pad.71 = f32[2,4,32,5,384]{4,1,3,2,0:T(4,128)} pad(f32[2,4,16,5,384]{4,1,3,2,0:T(4,128)} %add.315, f32[]{:T(128)} %constant.47.clone.1), padding=0_0_0x0_0_0x1_0_1x0_0_0x0_0_0 | pad | bytes 2949124 | tf_op jit(solution)/shard_map/pad | solution.py:48
  199.5 1.5 multiply_subtract_fusion.3
  202.1 49.6 %pad.70 = f32[2,4,32,5,384]{4,1,3,2,0:T(4,128)} pad(f32[2,4,16,5,384]{4,1,3,2,0:T(4,128)S(1)} %pad_maximum_fusion, f32[]{:T(128)} %constant.47.clone.1), padding=0_0_0x0_0_0x0_1_1x0_0_0x0_0_0 | pad | bytes 2949124 | tf_op jit(solution)/shard_map/pad | solution.py:48
  251.7 1.5 slice_add_fusion.8
  253.5 1.8 add_bitcast_fusion
  255.3 469.6 %all-gather.5.cloned.1.call-done = f32[512,1,1,5,384]{4,2,3,1,0:T(1,128)} async-done(((f32[2,1,1,5,384]{4,2,3,1,0:T(1,128)}), f32[512,1,1,5,384]{4,2,3,1,0:T(1,128)}) %all-gather.5.cloned.1.call-update) | async-done | bytes 3932176 | tf_op jit(solution)/shard_map/all_gather | solution.py:11
  724.9 731.3 %all-gather.7.cloned.1.call-done = f32[512,4,1,5,384]{4,1,3,2,0:T(4,128)} async-done(((f32[2,4,1,5,384]{4,1,3,2,0:T(4,128)}), f32[512,4,1,5,384]{4,1,3,2,0:T(4,128)}) %all-gather.7.cloned.1.call-update) | async-done | bytes 15728656 | tf_op jit(solution)/shard_map/all_gather | solution.py:11
  1456.2 440.8 %while.16 = (s32[]{:T(128)}, f32[2,1,5,384]{3,2,1,0:T(8,128)S(1)}, f32[2,4,5,384]{3,2,1,0:T(8,128)S(1)}, s32[]{:T(128)}, f32[256,2,1,5,384]{4,2,3,1,0:T(1,128)},...) while((s32[]{:T(128)}, f32[2,1,5,384]{3,2,1,0:T(8,128)S(1)}, ...), condition=%wide.region_1.2_spmd.clone, body=%wide.region_0.1_spmd.clone.sunk | while | flops 142085 | bytes 783507 | solution.py:20
  1457.0 0.8 constant_dynamic-slice_fusion.6
  1458.7 0.8 constant_dynamic-slice_fusion.6
  1460.5 0.8 constant_dynamic-slice_fusion.6
  1462.2 0.8 constant_dynamic-slice_fusion.6
  1463.9 0.8 constant_dynamic-slice_fusion.6
  1465.6 0.8 constant_dynamic-slice_fusion.6
  1467.4 0.8 constant_dynamic-slice_fusion.6
  1482.9 0.8 constant_dynamic-slice_fusion.6
  1484.7 0.8 constant_dynamic-slice_fusion.6
  1486.4 0.8 constant_dynamic-slice_fusion.6
  1488.1 0.8 constant_dynamic-slice_fusion.6
  1489.8 0.8 constant_dynamic-slice_fusion.6
  1491.6 0.8 constant_dynamic-slice_fusion.6
  1493.3 0.8 constant_dynamic-slice_fusion.6
  1495.0 0.8 constant_dynamic-slice_fusion.6
  1496.8 0.8 constant_dynamic-slice_fusion.6
  1498.5 0.8 constant_dynamic-slice_fusion.6
  1500.2 0.8 constant_dynamic-slice_fusion.6
  1515.8 0.8 constant_dynamic-slice_fusion.6
  1517.5 0.8 constant_dynamic-slice_fusion.6
  1519.2 0.8 constant_dynamic-slice_fusion.6
  1897.0 0.9 fusion.14
  1899.5 1.1 copy.107
  1900.7 239.8 %all-reduce.23.cloned.1.call-done = (f32[2,4,5,384]{3,1,2,0:T(4,128)}, f32[2,1,5,384]{3,0,2,1:T(2,128)}) async-done(((f32[2,4,5,384]{3,1,2,0:T(4,128)}, f32[2,1,5,384]{3,0,2,1:T(2,128)}), (f32[2,4,5,384]{3,1,2,0:T(4,128)}, f32[2,1,5,384]{3,0,2,1:T(2,128)})) %all-reduce.23.cloned.1.call-update) | async-done | bytes 76816 | tf_op jit(solution)/shard_map/psum | solution.py:25
  2140.5 0.9 multiply_add_fusion.21
  2142.7 0.9 maximum_add_fusion.1
  2143.6 1.5 copy.117
  (2167 shorter events, 425.7 us)
Async XLA Ops:
  6.5 718.4 %all-gather.5.cloned.1.call-start = ((), (), s32[]{:S(2)}) async-start(), calls=%async_computation | async-start | bytes 3947520 | tf_op jit(solution)/shard_map/all_gather | solution.py:11
  12.3 1.8 copy-start.4
  13.3 0.8 copy-start.6
  14.0 1442.2 %all-gather.7.cloned.1.call-start = ((), (), s32[]{:S(2)}) async-start(), calls=%async_computation.1 | async-start | bytes 15790080 | tf_op jit(solution)/shard_map/all_gather | solution.py:11
  18.6 3.2 copy-start.3
  21.8 26.6 %slice-start = ((f32[2,4,8,5,384]{4,1,3,2,0:T(4,128)}), f32[2,4,1,5,384]{4,1,3,2,0:T(4,128)S(1)}, s32[]{:S(2)}) async-start(f32[2,4,8,5,384]{4,1,3,2,0:T(4,128)} %copy-done.3), calls=%async_computation.3 | async-start | bytes 122880 | tf_op jit(solution)/shard_map/slice | solution.py:48
  22.2 7.8 copy-start.8
  30.0 0.7 copy-start.9
  68.1 3.4 copy-start.14
  71.3 29.3 %copy-start.7 = (f32[2,4,8,5,384]{4,1,3,2,0:T(4,128)S(1)}, f32[2,4,8,5,384]{4,1,3,2,0:T(4,128)}, u32[]{:S(2)}) copy-start(f32[2,4,8,5,384]{4,1,3,2,0:T(4,128)} %add.312) | copy-start | bytes 1474564
  128.2 71.2 %copy-start.12 = (f32[15,5,384]{2,0,1:T(8,128)S(1)}, f32[15,5,384]{2,0,1:T(8,128)}, u32[]{:S(2)}) copy-start(f32[15,5,384]{2,0,1:T(8,128)} %get-tuple-element.213) | copy-start | bytes 345604
  128.2 71.2 %copy-start.11 = (f32[15,5,384]{2,0,1:T(8,128)S(1)}, f32[15,5,384]{2,0,1:T(8,128)}, u32[]{:S(2)}) copy-start(f32[15,5,384]{2,0,1:T(8,128)} %get-tuple-element.212) | copy-start | bytes 345604
  201.0 0.8 copy-start.13
  202.1 49.6 %copy-start = (f32[2,4,32,5,384]{4,1,3,2,0:T(4,128)S(1)}, f32[2,4,32,5,384]{4,1,3,2,0:T(4,128)}, u32[]{:S(2)}) copy-start(f32[2,4,32,5,384]{4,1,3,2,0:T(4,128)} %pad.71) | copy-start | bytes 5898244
  202.1 51.4 %copy-start.5 = (f32[2,1,32,5,384]{4,2,3,1,0:T(8,128)S(1)}, f32[2,1,32,5,384]{4,2,3,1,0:T(8,128)}, u32[]{:S(2)}) copy-start(f32[2,1,32,5,384]{4,2,3,1,0:T(8,128)} %copy-done.4) | copy-start | bytes 1474564
  202.1 1254.1 %copy-start.2 = (f32[2,1,5,384]{3,2,1,0:T(8,128)S(1)}, f32[2,1,5,384]{3,2,1,0:T(8,128)}, u32[]{:S(2)}) copy-start(f32[2,1,5,384]{3,2,1,0:T(8,128)} %constant.49.clone.1) | copy-start | bytes 46084
  253.2 1887.2 %all-reduce.23.cloned.1.call-start = ((), (), s32[]{:S(2)}) async-start(), calls=%async_computation.2 | async-start | bytes 153600 | tf_op jit(solution)/shard_map/psum | solution.py:25
  1456.2 441.8 %copy-start.10 = (f32[2,4,1,5,384]{4,1,3,2,0:T(4,128)S(1)}, f32[2,4,1,5,384]{4,1,3,2,0:T(4,128)}, u32[]{:S(2)}) copy-start(f32[2,4,1,5,384]{4,1,3,2,0:T(4,128)} %slice_add_fusion.8) | copy-start | bytes 184324
  2140.5 2.2 copy-start.1
Sparse Core Ops, SparseCore 0:
  14.1 710.7 all-gather.4
  726.8 729.3 all-gather.6
  1899.5 240.9 all-reduce.22
where the time goes:
time: 2180 us; the launch traced here: 2150 us
  waiting for transfers between devices  1440 us (66%)
  local copies, waits for them, and re-layouts  627 us (29%)
  other arithmetic  54.5 us (2%)
    all_gather x2, waiting for transfers between devices, carried_in(): pieces = jax.tree.map(lambda part: lax.all_gather(part, axis), value)  1200 us
    psum x1, waiting for transfers between devices, broadcast(): return lax.psum(kept, axis)  240 us
    pad x16, local copies, waits for them, and re-layouts, local(): local_a, local_b = lax.associative_scan(compose, (coeff, source), axis=2)  216 us
    dynamic_slice x255, local copies, waits for them, and re-layouts, hop(): longer = join(subtotal, jax.tree.map(lambda part: part[position], pieces))  215 us
    slice x255, local copies, waits for them, and re-layouts, complex_product(): left[1] * right[1]  185 us
  transfers between devices with their start and end apart: 3, of which 3 were waited for; matrix products, arithmetic and copies ran while one was open for 11% of the time, Pallas kernels for 0%

commit v1 on v0

--- a/solution.py
+++ b/solution.py
@@ -4,6 +4,12 @@
 from jax.sharding import PartitionSpec as P
 
 fringe_total = 0.7
+
+
+def gather_and_add(array, axis):
+    parts = lax.all_gather(array, axis, axis=0, tiled=False)
+    total = parts.sum(axis=0)
+    return total
 
 
 def carried_in(value, axis, join, neutral):
@@ -22,7 +28,7 @@
 
 def broadcast(value, axis, source):
     kept = jnp.where(lax.axis_index(axis) == source, value, 0).astype(value.dtype)
-    return lax.psum(kept, axis)
+    return gather_and_add(kept, axis)
 
 
 def complex_product(left, right):

time: 2180 us -> 3390 us (1.56)
  waiting for transfers between devices: 1440 us -> 2640 us
    all_gather x0 -> x2, waiting for transfers between devices: none -> 1430 us  [gather_and_add(): parts = lax.all_gather(array, axis, axis=0, tiled=False)]
    psum x1 -> x0, waiting for transfers between devices: 240 us -> none  [broadcast(): return lax.psum(kept, axis)]
  transfers between devices with their start and end apart: 3 -> 4, of which waited for: 3 -> 4; matrix products, arithmetic and copies ran while one was open for 11% -> 7% of each run, Pallas kernels for 0% -> 0%
where the time goes in v1:
time: 3390 us; the launch traced here: 3350 us
  waiting for transfers between devices  2640 us (78%)
  local copies, waits for them, and re-layouts  627 us (18%)
  other arithmetic  61.3 us (2%)
    all_gather x2, waiting for transfers between devices, gather_and_add(): parts = lax.all_gather(array, axis, axis=0, tiled=False)  1430 us
    all_gather x2, waiting for transfers between devices, carried_in(): pieces = jax.tree.map(lambda part: lax.all_gather(part, axis), value)  1200 us
    pad x16, local copies, waits for them, and re-layouts, local(): local_a, local_b = lax.associative_scan(compose, (coeff, source), axis=2)  216 us
    dynamic_slice x255, local copies, waits for them, and re-layouts, hop(): longer = join(subtotal, jax.tree.map(lambda part: part[position], pieces))  215 us
    slice x255, local copies, waits for them, and re-layouts, complex_product(): left[1] * right[1]  185 us
  transfers between devices with their start and end apart: 4, of which 4 were waited for; matrix products, arithmetic and copies ran while one was open for 7% of the time, Pallas kernels for 0%

profile of v1, /device:TPU:1, one launch (start us, length us, event | category | flops | bytes accessed | tf_op | source)
XLA Modules:
  0.0 3354.5 jit_solution(15454094883601345141)
XLA Ops:
  6.5 2.1 multiply_bitcast_fusion.1
  14.2 2.9 copy_multiply_fusion
  22.8 7.1 pad.65
  31.3 14.1 pad.67
  46.2 1.1 multiply_subtract_fusion.9
  47.3 1.0 maximum_add_fusion.7
  49.1 18.9 pad.66
  68.0 1.9 add.318
  69.9 1.3 multiply_subtract_fusion.5
  71.4 0.9 pad_maximum_fusion.1
  72.3 28.2 pad.68
  100.5 25.2 pad.69
  125.7 2.4 add.321
  128.1 71.2 %pad.71 = f32[2,4,32,5,384]{4,1,3,2,0:T(4,128)} pad(f32[2,4,16,5,384]{4,1,3,2,0:T(4,128)} %add.321, f32[]{:T(128)} %constant.47.clone.1), padding=0_0_0x0_0_0x1_0_1x0_0_0x0_0_0 | pad | bytes 2949124 | tf_op jit(solution)/shard_map/pad | solution.py:54
  199.4 1.5 multiply_subtract_fusion.3
  202.0 49.6 %pad.70 = f32[2,4,32,5,384]{4,1,3,2,0:T(4,128)} pad(f32[2,4,16,5,384]{4,1,3,2,0:T(4,128)S(1)} %pad_maximum_fusion, f32[]{:T(128)} %constant.47.clone.1), padding=0_0_0x0_0_0x0_1_1x0_0_0x0_0_0 | pad | bytes 2949124 | tf_op jit(solution)/shard_map/pad | solution.py:54
  251.7 1.5 slice_add_fusion.8
  253.2 471.7 %all-gather.11.cloned.1.call-done = f32[512,1,1,5,384]{4,2,3,1,0:T(1,128)} async-done(((f32[2,1,1,5,384]{4,2,3,1,0:T(1,128)}), f32[512,1,1,5,384]{4,2,3,1,0:T(1,128)}) %all-gather.11.cloned.1.call-update) | async-done | bytes 3932176 | tf_op jit(solution)/shard_map/all_gather | solution.py:17
  724.9 731.3 %all-gather.13.cloned.1.call-done = f32[512,4,1,5,384]{4,1,3,2,0:T(4,128)} async-done(((f32[2,4,1,5,384]{4,1,3,2,0:T(4,128)}), f32[512,4,1,5,384]{4,1,3,2,0:T(4,128)}) %all-gather.13.cloned.1.call-update) | async-done | bytes 15728656 | tf_op jit(solution)/shard_map/all_gather | solution.py:17
  1456.2 440.9 %while.16 = (s32[]{:T(128)}, f32[2,1,5,384]{3,2,1,0:T(8,128)S(1)}, f32[2,4,5,384]{3,2,1,0:T(8,128)S(1)}, s32[]{:T(128)}, f32[256,2,1,5,384]{4,2,3,1,0:T(1,128)},...) while((s32[]{:T(128)}, f32[2,1,5,384]{3,2,1,0:T(8,128)S(1)}, ...), condition=%wide.region_1.2_spmd.clone, body=%wide.region_0.1_spmd.clone.sunk | while | flops 142085 | bytes 783507 | solution.py:26
  1457.1 0.8 constant_dynamic-slice_fusion.6
  1458.8 0.8 constant_dynamic-slice_fusion.6
  1460.6 0.8 constant_dynamic-slice_fusion.6
  1462.3 0.8 constant_dynamic-slice_fusion.6
  1464.0 0.8 constant_dynamic-slice_fusion.6
  1467.5 0.8 constant_dynamic-slice_fusion.6
  1469.2 0.8 constant_dynamic-slice_fusion.6
  1470.9 0.8 constant_dynamic-slice_fusion.6
  1472.7 0.8 constant_dynamic-slice_fusion.6
  1474.4 0.8 constant_dynamic-slice_fusion.6
  1476.1 0.8 constant_dynamic-slice_fusion.6
  1477.8 0.8 constant_dynamic-slice_fusion.6
  1479.6 0.8 constant_dynamic-slice_fusion.6
  1481.3 0.8 constant_dynamic-slice_fusion.6
  1483.0 0.8 constant_dynamic-slice_fusion.6
  1484.8 0.8 constant_dynamic-slice_fusion.6
  1500.3 0.8 constant_dynamic-slice_fusion.6
  1502.0 0.8 constant_dynamic-slice_fusion.6
  1503.8 0.8 constant_dynamic-slice_fusion.6
  1505.5 0.8 constant_dynamic-slice_fusion.6
  1507.2 0.8 constant_dynamic-slice_fusion.6
  1899.3 705.2 %all-gather.9.cloned.1.call-done = f32[256,2,1,5,384]{4,1,3,2,0:T(2,128)} async-done(((f32[1,2,1,5,384]{4,1,3,2,0:T(2,128)}), f32[256,2,1,5,384]{4,1,3,2,0:T(2,128)}) %all-gather.9.cloned.1.call-update) | async-done | bytes 3932176 | tf_op jit(solution)/shard_map/all_gather | solution.py:10
  2604.5 3.2 reduce_sum.19
  2607.8 727.8 %all-gather.7.cloned.1.call-done = f32[256,2,4,5,384]{4,2,3,1,0:T(4,128)} async-done(((f32[1,2,4,5,384]{4,2,3,1,0:T(4,128)}), f32[256,2,4,5,384]{4,2,3,1,0:T(4,128)}) %all-gather.7.cloned.1.call-update) | async-done | bytes 15728656 | tf_op jit(solution)/shard_map/all_gather | solution.py:10
  3335.6 8.4 reduce_sum.18
  3344.6 1.0 copy-done.1
  3345.6 0.9 maximum_add_fusion.1
  3346.5 1.5 copy.160
  (2175 shorter events, 425.3 us)
Async XLA Ops:
  6.5 718.4 %all-gather.11.cloned.1.call-start = ((), (), s32[]{:S(2)}) async-start(), calls=%async_computation.2 | async-start | bytes 3947520 | tf_op jit(solution)/shard_map/all_gather | solution.py:17
  12.2 1.8 copy-start.4
  13.3 0.8 copy-start.6
  14.0 1442.2 %all-gather.13.cloned.1.call-start = ((), (), s32[]{:S(2)}) async-start(), calls=%async_computation.3 | async-start | bytes 15790080 | tf_op jit(solution)/shard_map/all_gather | solution.py:17
  18.6 3.1 copy-start.3
  21.8 26.6 slice-start
  22.1 7.8 copy-start.9
  29.9 0.7 copy-start.10
  68.0 3.4 copy-start.15
  71.2 29.3 copy-start.8
  128.1 71.2 %copy-start.13 = (f32[15,5,384]{2,0,1:T(8,128)S(1)}, f32[15,5,384]{2,0,1:T(8,128)}, u32[]{:S(2)}) copy-start(f32[15,5,384]{2,0,1:T(8,128)} %get-tuple-element.217) | copy-start | bytes 345604
  128.1 71.2 %copy-start.12 = (f32[15,5,384]{2,0,1:T(8,128)S(1)}, f32[15,5,384]{2,0,1:T(8,128)}, u32[]{:S(2)}) copy-start(f32[15,5,384]{2,0,1:T(8,128)} %get-tuple-element.216) | copy-start | bytes 345604
  200.9 0.8 copy-start.14
  202.0 49.7 %copy-start = (f32[2,4,32,5,384]{4,1,3,2,0:T(4,128)S(1)}, f32[2,4,32,5,384]{4,1,3,2,0:T(4,128)}, u32[]{:S(2)}) copy-start(f32[2,4,32,5,384]{4,1,3,2,0:T(4,128)} %pad.71) | copy-start | bytes 5898244
  202.0 1254.2 %copy-start.2 = (f32[2,1,5,384]{3,2,1,0:T(8,128)S(1)}, f32[2,1,5,384]{3,2,1,0:T(8,128)}, u32[]{:S(2)}) copy-start(f32[2,1,5,384]{3,2,1,0:T(8,128)} %constant.49.clone.1) | copy-start | bytes 46084
  253.2 2351.3 %all-gather.9.cloned.1.call-start = ((), (), s32[]{:S(2)}) async-start(), calls=%async_computation.1 | async-start | bytes 3947520 | tf_op jit(solution)/shard_map/all_gather | solution.py:10
  1456.2 440.9 %copy-start.5 = (f32[2,1,32,5,384]{4,2,3,1,0:T(8,128)S(1)}, f32[2,1,32,5,384]{4,2,3,1,0:T(8,128)}, u32[]{:S(2)}) copy-start(f32[2,1,32,5,384]{4,2,3,1,0:T(8,128)} %copy-done.4) | copy-start | bytes 1474564
  1456.2 440.9 %copy-start.7 = (f32[2,1,32,5,384]{4,2,3,1,0:T(8,128)S(1)}, f32[2,1,32,5,384]{4,2,3,1,0:T(8,128)}, u32[]{:S(2)}) copy-start(f32[2,1,32,5,384]{4,2,3,1,0:T(8,128)} %copy-done.6) | copy-start | bytes 1474564
  1456.2 442.0 %copy-start.11 = (f32[2,4,1,5,384]{4,1,3,2,0:T(4,128)S(1)}, f32[2,4,1,5,384]{4,1,3,2,0:T(4,128)}, u32[]{:S(2)}) copy-start(f32[2,4,1,5,384]{4,1,3,2,0:T(4,128)} %slice_add_fusion.8) | copy-start | bytes 184324
  1897.9 1437.7 %all-gather.7.cloned.1.call-start = ((), (), s32[]{:S(2)}) async-start(), calls=%async_computation | async-start | bytes 15790080 | tf_op jit(solution)/shard_map/all_gather | solution.py:10
  3344.1 1.5 copy-start.1
Sparse Core Ops, SparseCore 0:
  14.1 710.7 all-gather.10
  726.8 729.3 all-gather.12
  1898.0 706.4 all-gather.8
  2606.2 729.3 all-gather.6
